TPU v7x, 32 devices: a whole 2x2x4 slice. The times are simulated.
32 devices in a mesh: member: 4 (over y, x), lon: 8 (over z, core).
Axes of the slice: x: 2, y: 2, z: 4, core: 2. Of those that a mesh axis runs over, the one named last changes fastest.
Arguments:
- fields: bfloat16 [4, 641, 20, 360], P('member', None, None, 'lon'), may hold values from -6 to 6
- weight: bfloat16 [5, 5, 73, 641], replicated, may hold values from -0.046875 to 0.046875
- out_bias: float32 [73], replicated, may hold values from -3 to 3
- observed: float32 [73, 16, 360], P(None, None, 'lon'), may hold values from -6 to 6
- widths: float32 [73], replicated, may hold values from 0.5 to 2
- owner_start: int32 [8, 5], P('lon'), may hold values from 0 to 16, as said below
Outputs:
- out_grad: bfloat16 [4, 73, 16, 360], P('member', None, None, 'lon')
- owned_score: float32 [8, 4, 540], P('lon', 'member')
- weight_grad: float32 [5, 5, 73, 641], replicated
- bias_grad: float32 [73], replicated
Inputs may be any that keep to these rules, and one draw needn't show every extreme that they name: Each row owner_start[l] starts at 0, never falls and ends at 16; owner r of longitude group l holds blocks owner_start[l, r] to owner_start[l, r + 1] - 1, at most 12 of them, and in every group some owner holds exactly 12.
All inputs are finite; a program needn't handle non-finite values.
Results may differ from a plain program's by a relative error of at most 0.0063.
Values may be sent and summed in bfloat16 or wider, within the bound.
No kernel may reach another device: no remote copies, remote signals or barrier semaphores. Data moves between devices by JAX's collectives and lax.ppermute only.
A program may use at most 128 MiB of HBM per device.

v0:
```python
import math
import jax
import jax.numpy as jnp
from jax import lax
from jax.sharding import PartitionSpec as P

BLOCK = 45


def extended(block, sides, width):
    for axis, dim in sides:
        count = lax.axis_size(axis)
        forward = [(i, i + 1) for i in range(count - 1)]
        forward.append((count - 1, 0))
        backward = [(target, source) for source, target in forward]
        low = lax.ppermute(
            lax.slice_in_dim(block, block.shape[dim] - width, None, axis=dim), axis, forward
        )
        high = lax.ppermute(lax.slice_in_dim(block, 0, width, axis=dim), axis, backward)
        block = jnp.concatenate([low, block, high], axis=dim)
    return block


def kernel_terms(values, target, widths):
    members = values.astype(jnp.float32)
    ensemble = members.shape[0]
    inverse = (1.0 / (widths * widths))[:, None]
    spread = members[:, None] - members[None, :]
    kernel_pair = jnp.exp(-0.5 * spread * spread * inverse)
    misfit = members - target[None]
    kernel_obs = jnp.exp(-0.5 * misfit * misfit * inverse)
    per_channel = (
        jnp.sum(kernel_pair, axis=(0, 1)) / (2.0 * ensemble * ensemble)
        - jnp.sum(kernel_obs, axis=0) / ensemble
    )
    scores = jnp.mean(per_channel, axis=0)
    gradient = inverse * (misfit * kernel_obs - jnp.sum(kernel_pair * spread, axis=1) / ensemble)
    return (scores, gradient.astype(jnp.bfloat16))


def tap_stack(gradients, rows_in, padded_width):
    leading = gradients.ndim - 2
    padded = jnp.pad(gradients, [(0, 0)] * leading + [(4, 4), (4, 4)])
    pieces = [
        padded[..., 4 - row_tap : 4 - row_tap + rows_in, 4 - col_tap : 4 - col_tap + padded_width]
        for row_tap in range(5)
        for col_tap in range(5)
    ]
    return jnp.stack(pieces, axis=-4)


def body(fields, weight, out_bias, observed, widths, owner_start):
    local_members, in_chan, rows_in, lon_dev = fields.shape
    out_chan = weight.shape[2]
    rows_out = rows_in - 4
    padded_width = lon_dev + 4
    padded = extended(fields, (("lon", 3),), 2)
    flat_field = padded.reshape(local_members, in_chan, rows_in * padded_width)
    flat_weight = weight.reshape(25 * out_chan, in_chan)
    tap_sums = jnp.einsum(
        "kc,mcp->mkp", flat_weight, flat_field, preferred_element_type=jnp.float32
    )
    tap_sums = tap_sums.reshape(local_members, 5, 5, out_chan, rows_in, padded_width)
    convolved = jnp.broadcast_to(
        out_bias[None, :, None, None], (local_members, out_chan, rows_out, lon_dev)
    )
    for row_tap in range(5):
        for col_tap in range(5):
            convolved = (
                convolved
                + tap_sums[
                    :,
                    row_tap,
                    col_tap,
                    :,
                    row_tap : row_tap + rows_out,
                    col_tap : col_tap + lon_dev,
                ]
            )
    outputs = convolved.astype(jnp.bfloat16)
    owners = lax.axis_size("member")
    own_rank = lax.axis_index("member")
    blocks = rows_out * lon_dev // BLOCK
    capacity = max(2, 3 * blocks // owners)
    starts = owner_start[0]
    slot_index = jnp.arange(capacity, dtype=jnp.int32)
    owned_blocks = starts[1:] - starts[:-1]
    filled = slot_index[None, :] < owned_blocks[:, None]
    global_block = starts[:-1, None] + slot_index[None, :]
    even_blocks = blocks // owners
    sending = outputs.reshape(local_members, out_chan, owners, even_blocks * BLOCK)
    arrived = lax.all_to_all(sending, "member", split_axis=2, concat_axis=0, tiled=True).reshape(
        -1, out_chan, even_blocks * BLOCK
    )
    target = lax.dynamic_slice_in_dim(observed, own_rank * even_blocks, even_blocks, 1)
    target = target.reshape(out_chan, even_blocks * BLOCK)
    scores, gradients = kernel_terms(arrived, target, widths)
    local_grad = lax.all_to_all(
        gradients.reshape(-1, out_chan, 1, even_blocks * BLOCK),
        "member",
        split_axis=0,
        concat_axis=2,
        tiled=True,
    )
    from_self = filled & (global_block // even_blocks == own_rank)
    local_index = jnp.clip(global_block - own_rank * even_blocks, 0, even_blocks - 1)
    parcel = jnp.take(scores.reshape(even_blocks, BLOCK), local_index.reshape(-1), axis=0)
    parcel = jnp.where(from_self[..., None], parcel.reshape(owners, capacity, BLOCK), 0.0)
    gathered = lax.all_to_all(
        parcel.reshape(owners, capacity * BLOCK), "member", split_axis=0, concat_axis=0, tiled=True
    )
    owned_score = jnp.sum(gathered, axis=0).reshape(1, 1, capacity * BLOCK)
    out_grad = local_grad.reshape(local_members, out_chan, rows_out, lon_dev)
    stacked = tap_stack(out_grad, rows_in, padded_width).reshape(
        local_members, 25 * out_chan, rows_in * padded_width
    )
    weight_part = lax.dot_general(
        stacked, flat_field, (((0, 2), (0, 2)), ((), ())), preferred_element_type=jnp.float32
    )
    bias_part = jnp.sum(out_grad.astype(jnp.float32), axis=(0, 2, 3))
    factor = 1.0 / math.sqrt(local_members * owners * rows_out * lon_dev * lax.axis_size("lon"))
    weight_sum, bias_sum = lax.psum((weight_part, bias_part), ("member", "lon"))
    weight_grad = (weight_sum * factor).reshape(5, 5, out_chan, in_chan)
    bias_grad = bias_sum * factor
    return (out_grad, owned_score, weight_grad, bias_grad)


def solution(mesh):
    in_specs = (P("member", None, None, "lon"), P(), P(), P(None, None, "lon"), P(), P("lon", None))
    out_specs = (P("member", None, None, "lon"), P("lon", "member", None), P(), P())
    return jax.shard_map(body, mesh=mesh, in_specs=in_specs, out_specs=out_specs, check_vma=False)
```

profile of v0, /device:TPU:0, one launch (start us, length us, event | category | flops | bytes accessed | tf_op | source)
XLA Modules:
  0.0 309.2 jit_solution(13475572679389987868)
XLA Ops:
  7.2 1.2 fusion.72
  8.4 0.5 collective-permute-start
  8.9 4.1 %collective-permute-start.1 = (bf16[1,641,20,2]{1,3,2,0:T(2,128)(2,1)S(1)}, bf16[1,641,20,2]{1,3,2,0:T(2,128)(2,1)S(1)}, u32[]{:S(2)}, u32[]{:S(2)}) collective-permute-start(bf16[1,641,20,2]{1,3,2,0:T(2,128)(2,1)S(1)} %get-tuple-element.56), channel_id=1, source_target_pairs={{1,0},{2,1},{3,2},{4,3},{5,4},{6,5},{7,6},{0,7},{9,8},{10,9},{11,1... | collective-permute-start | bytes 153848 | tf_op jit(solution)/shard_map/ppermute | solution.py:19
  13.0 0.7 multiply_divide_fusion
  13.7 4.9 %reshape.609 = bf16[1825,641]{1,0:T(8,128)(2,1)} reshape(bf16[5,5,73,641]{3,2,1,0:T(8,128)(2,1)} %param.7) | data formatting | bytes 4679300 | tf_op jit(solution)/shard_map/reshape | solution.py:59
  18.6 2.4 pad_maximum_fusion
  21.0 1.9 reshape.608
  22.9 8.4 %convolution_bitcast_fusion = f32[1,1825,980]{2,1,0:T(8,128)} fusion(bf16[641,980]{0,1:T(8,128)(2,1)} %reshape.608, bf16[1825,641]{1,0:T(8,128)(2,1)} %reshape.609), kind=kOutput, calls=%fused_computation.1 | convolution fusion | flops 2292857088 | bytes 10750010 | tf_op jit(solution)/shard_map/kc,mcp->mkp/dot_general | solution.py:60
  31.2 8.7 %copy.47 = f32[1,1825,980]{1,2,0:T(8,128)} copy(f32[1,1825,980]{2,1,0:T(8,128)} %convolution_bitcast_fusion) | data formatting | bytes 14308000 | tf_op jit(solution)/shard_map/kc,mcp->mkp/transpose | solution.py:60
  39.9 14.5 %reshape.610 = f32[1,5,5,73,20,49]{3,2,1,5,4,0:T(8,128)} reshape(f32[1,1825,980]{1,2,0:T(8,128)} %copy.47) | data formatting | bytes 14308000 | tf_op jit(solution)/shard_map/reshape | solution.py:63
  54.5 22.3 %fusion.70 = (f32[1,1,1,73,16,45]{3,2,1,5,4,0:T(1,128)S(1)}, f32[1,1,1,73,16,45]{3,2,1,5,4,0:T(1,128)S(1)}, f32[1,1,1,73,16,45]{3,2,1,5,4,0:T(1,128)S(1)}, f32[1...) fusion(f32[1,5,5,73,20,49]{3,2,1,5,4,0:T(8,128)} %reshape.610), kind=kLoop, calls=%fused_computation.130 | loop fusion | bytes 7989120 | tf_op jit(solution)/shard_map/slice | solution.py:71
  76.8 9.1 %fusion.71 = (f32[1,1,1,73,16,45]{3,2,1,5,4,0:T(1,128)S(1)}, f32[1,1,1,73,16,45]{3,2,1,5,4,0:T(1,128)S(1)}, f32[1,1,1,73,16,45]{3,2,1,5,4,0:T(1,128)S(1)}, f32[1...) fusion(f32[1,5,5,73,20,49]{3,2,1,5,4,0:T(8,128)} %reshape.610), kind=kLoop, calls=%fused_computation.131 | loop fusion | bytes 2522880 | tf_op jit(solution)/shard_map/slice | solution.py:71
  85.9 3.6 %add_convert_fusion = bf16[1,73,4,180]{1,0,3,2:T(2,128)(2,1)S(1)} fusion(f32[1,73,4,180]{1,0,3,2:T(1,128)S(1)} %bitcast.193, f32[1,73,4,180]{1,0,3,2:T(1,128)S(1)} %bitcast.194, f32[1,73,4,180]{1,0,3,2:T(1,128)S(1)} %bitcast.195, f32[1,73,4,180]{1,0,3,2:T(1,128)S(1)} %bitcast.196, f32[1,73,4,180]{1,0,3,2:T(1,128)S(1)} %bitcast.197, ...), kind=kLoop, calls=%fused_computation.38 | loop fusion | flops 1366560 | bytes 5361412 | tf_op jit(solution)/shard_map/convert_element_type | solution.py:80
  89.5 1.0 copy.48
  90.4 4.2 %all-to-all-start = ((bf16[1,73,4,180]{3,1,0,2:T(8,128)(2,1)}), bf16[1,73,4,180]{3,1,0,2:T(8,128)(2,1)S(1)}, u32[]{:S(2)}, u32[]{:S(2)}) async-start(bf16[1,73,4,180]{3,1,0,2:T(8,128)(2,1)} %copy.48), calls=%async_computation | async-start | bytes 327680 | tf_op jit(solution)/shard_map/all_to_all | solution.py:92
  94.6 0.1 copy.62
  94.8 0.1 reshape.627
  94.9 4.8 %all-to-all-done = bf16[1,73,4,180]{3,1,0,2:T(8,128)(2,1)S(1)} async-done(((bf16[1,73,4,180]{3,1,0,2:T(8,128)(2,1)}), bf16[1,73,4,180]{3,1,0,2:T(8,128)(2,1)S(1)}, u32[]{:S(2)}, u32[]{:S(2)}) %all-to-all-start) | async-done | bytes 105152 | tf_op jit(solution)/shard_map/all_to_all | solution.py:92
  99.7 0.4 fusion.11
  100.2 1.6 fusion.3
  101.9 0.5 fusion.13
  102.4 7.8 %all_to_all.30 = bf16[4,73,1,180]{3,1,2,0:T(8,128)(2,1)S(1)} all-to-all(bf16[4,73,1,180]{3,1,2,0:T(8,128)(2,1)S(1)} %copy.54), channel_id=1, replica_groups=mesh['member'=4,'lon'=8] {'member'}, dimensions={0} | all-to-all | bytes 210240 | tf_op jit(solution)/shard_map/all_to_all | solution.py:98
  110.2 0.6 convert_reduce_fusion
  110.8 0.2 copy.56
  111.2 0.1 fusion.17
  111.3 0.1 fusion.19
  111.4 0.1 fusion.21
  111.5 0.1 fusion.23
  111.7 0.1 fusion.27
  111.8 0.1 fusion.29
  111.9 0.1 fusion.31
  112.0 0.1 fusion.33
  112.1 0.1 fusion.35
  112.2 0.1 fusion.37
  112.3 0.1 fusion.39
  112.4 0.1 fusion.41
  112.5 0.1 fusion.43
  112.7 0.1 fusion.47
  112.8 0.1 fusion.49
  112.9 0.1 fusion.51
  113.0 0.1 fusion.53
  113.2 0.1 fusion.57
  113.3 0.1 fusion.59
  113.4 0.1 fusion.61
  113.5 0.1 fusion.63
  113.6 5.8 %copy.59 = bf16[1,25,73,20,49]{2,1,4,3,0:T(8,128)(2,1)} copy(bf16[1,25,73,20,49]{2,4,3,1,0:T(8,128)(2,1)S(1)} %fusion.63) | data formatting | bytes 7154000 | tf_op jit(solution)/shard_map/stack | solution.py:49
  119.5 13.7 %reshape.613 = bf16[1825,980]{0,1:T(8,128)(2,1)} reshape(bf16[1,25,73,20,49]{2,1,4,3,0:T(8,128)(2,1)} %copy.59) | data formatting | bytes 7154000 | tf_op jit(solution)/shard_map/reshape.9
  133.2 7.4 %fusion.73 = f32[1825,641]{0,1:T(8,128)} fusion(bf16[1825,980]{0,1:T(8,128)(2,1)} %reshape.613, bf16[641,980]{0,1:T(8,128)(2,1)S(1)} %copy-done.2), kind=kOutput, calls=%fused_computation.133 | convolution fusion | flops 2292857088 | bytes 9512660 | tf_op jit(solution)/shard_map/dot_general | solution.py:117
  140.7 0.1 min.9
  140.8 0.1 compare_and_fusion
  141.0 0.1 broadcast_in_dim.41
  141.2 0.1 broadcast_in_dim.43
  141.4 0.1 div.61
  141.4 0.6 gather_fusion
  142.0 0.1 gather.7
  142.2 7.2 %all_to_all.31 = f32[4,1,540]{2,1,0:T(1,128)S(1)} all-to-all(f32[4,1,540]{2,1,0:T(1,128)S(1)} %copy.58), channel_id=1, replica_groups=mesh['member'=4,'lon'=8] {'member'}, dimensions={0} | all-to-all | bytes 17280 | tf_op jit(solution)/shard_map/all_to_all | solution.py:109
  149.4 0.6 reshape.612
  150.0 0.7 copy.61
  150.7 38.1 %psum.15 = f32[73]{0:T(128)S(1)} all-reduce(f32[73]{0:T(128)S(1)} %get-tuple-element.26), channel_id=1, replica_groups=mesh['member'=4,'lon'=8] {'member','lon'}, use_global_device_ids=true, to_apply=%region_7.8 | all-reduce | flops 73 | bytes 584 | tf_op jit(solution)/shard_map/psum | solution.py:122
  188.8 0.5 broadcast_multiply_fusion.3
  189.3 95.6 %all-reduce.3.cloned.1.call-done = f32[1825,641]{0,1:T(8,128)} async-done(((f32[1825,641]{0,1:T(8,128)}), f32[1825,641]{0,1:T(8,128)}) %all-reduce.3.cloned.1.call-update) | async-done | bytes 4679316 | tf_op jit(solution)/shard_map/psum | solution.py:122
  284.9 5.1 %broadcast_multiply_fusion = f32[1825,641]{0,1:T(8,128)} fusion(f32[1825,641]{0,1:T(8,128)} %all-reduce.3.cloned.1.call-done), kind=kLoop, calls=%fused_computation.2 | loop fusion | flops 1169825 | bytes 9358600 | tf_op jit(solution)/shard_map/mul | solution.py:123
  290.0 6.1 %copy.60 = f32[1825,641]{1,0:T(8,128)} copy(f32[1825,641]{0,1:T(8,128)} %broadcast_multiply_fusion) | data formatting | bytes 9358600 | tf_op jit(solution)/shard_map/mul | solution.py:123
  296.1 6.2 %reshape.614 = f32[5,5,73,641]{3,2,1,0:T(8,128)} reshape(f32[1825,641]{1,0:T(8,128)} %copy.60) | data formatting | bytes 9358600 | tf_op jit(solution)/shard_map/reshape | solution.py:123
  (36 shorter events, 0.9 us)
Async XLA Ops:
  7.2 87.4 %copy-start = (f32[73,16,45]{0,1,2:T(8,128)S(1)}, f32[73,16,45]{0,1,2:T(8,128)}, u32[]{:S(2)}) copy-start(f32[73,16,45]{0,1,2:T(8,128)} %param.9) | copy-start | bytes 630724
  8.4 10.2 %collective-permute-start = (bf16[1,641,20,2]{1,3,2,0:T(2,128)(2,1)S(1)}, bf16[1,641,20,2]{1,3,2,0:T(2,128)(2,1)S(1)}, u32[]{:S(2)}, u32[]{:S(2)}) collective-permute-start(bf16[1,641,20,2]{1,3,2,0:T(2,128)(2,1)S(1)} %get-tuple-element.55), channel_id=1, source_target_pairs={{0,1},{1,2},{2,3},{3,4},{4,5},{5,6},{6,7},{7,0},{8,9},{9,10},{10,1... | collective-permute-start | bytes 153848 | tf_op jit(solution)/shard_map/ppermute | solution.py:16
  8.9 9.7 %collective-permute-start.1 = (bf16[1,641,20,2]{1,3,2,0:T(2,128)(2,1)S(1)}, bf16[1,641,20,2]{1,3,2,0:T(2,128)(2,1)S(1)}, u32[]{:S(2)}, u32[]{:S(2)}) collective-permute-start(bf16[1,641,20,2]{1,3,2,0:T(2,128)(2,1)S(1)} %get-tuple-element.56), channel_id=1, source_target_pairs={{1,0},{2,1},{3,2},{4,3},{5,4},{6,5},{7,6},{0,7},{9,8},{10,9},{11,1... | collective-permute-start | bytes 153848 | tf_op jit(solution)/shard_map/ppermute | solution.py:19
  54.5 31.4 %copy-start.3 = (f32[73]{0:T(128)S(1)}, f32[73]{0:T(128)}, u32[]{:S(2)}) copy-start(f32[73]{0:T(128)} %param.8) | copy-start | bytes 880
  90.4 9.3 %all-to-all-start = ((bf16[1,73,4,180]{3,1,0,2:T(8,128)(2,1)}), bf16[1,73,4,180]{3,1,0,2:T(8,128)(2,1)S(1)}, u32[]{:S(2)}, u32[]{:S(2)}) async-start(bf16[1,73,4,180]{3,1,0,2:T(8,128)(2,1)} %copy.48), calls=%async_computation | async-start | bytes 327680 | tf_op jit(solution)/shard_map/all_to_all | solution.py:92
  94.6 190.3 %all-reduce.3.cloned.1.call-start = ((), (), s32[]{:S(2)}) async-start(), calls=%async_computation.3 | async-start | bytes 9953280 | tf_op jit(solution)/shard_map/psum | solution.py:122
  119.5 13.7 %copy-start.2 = (bf16[641,980]{0,1:T(8,128)(2,1)S(1)}, bf16[641,980]{0,1:T(8,128)(2,1)}, u32[]{:S(2)}) copy-start(bf16[641,980]{0,1:T(8,128)(2,1)} %reshape.608) | copy-start | bytes 3769084
  133.2 7.4 %copy-start.4 = (s32[1,5]{1,0:T(1,128)S(1)}, s32[1,5]{1,0:T(1,128)}, u32[]{:S(2)}) copy-start(s32[1,5]{1,0:T(1,128)} %param.11) | copy-start | bytes 64
  290.0 12.3 %copy-start.1 = (f32[73,16,45]{0,1,2:T(8,128)S(1)}, f32[73,16,45]{0,1,2:T(8,128)}, u32[]{:S(2)}) copy-start(f32[73,16,45]{0,1,2:T(8,128)} %param.9) | copy-start | bytes 630724
Sparse Core Ops, SparseCore 0:
  140.7 144.1 all-reduce.2
where the time goes:
time: 311 us; the launch traced here: 309 us
  local copies, waits for them, and re-layouts  101 us (32%)
  waiting for transfers between devices  100 us (32%)
  blocking collectives  53.1 us (17%)
  other arithmetic  15.7 us (5%)
  matrix products  15.7 us (5%)
  between operations  14.3 us (5%)
  starting transfers between devices  8.79 us (3%)
    psum x1, waiting for transfers between devices, body(): weight_sum, bias_sum = lax.psum((weight_part, bias_part), ('member', 'lon'))  95.6 us
    psum x1, blocking collectives, body(): weight_sum, bias_sum = lax.psum((weight_part, bias_part), ('member', 'lon'))  38.1 us
    slice x2, local copies, waits for them, and re-layouts, body(): tap_sums[:, row_tap, col_tap, :, row_tap:row_tap + rows_out, col_tap:col_...  31.4 us
    another operation x2, local copies, waits for them, and re-layouts  15.6 us
    reshape x1, local copies, waits for them, and re-layouts, body(): tap_sums.reshape(local_members, 5, 5, out_chan, rows_in, padded_width)  14.5 us
    transpose x1, local copies, waits for them, and re-layouts, body(): jnp.einsum('kc,mcp->mkp', flat_weight, flat_field, preferred_element_type...  8.69 us
    dot_general x1, matrix products, body(): jnp.einsum('kc,mcp->mkp', flat_weight, flat_field, preferred_element_type...  8.37 us
    all_to_all x1, blocking collectives, body(): lax.all_to_all(gradients.reshape(-1, out_chan, 1, even_blocks * BLOCK), '...  7.82 us
  transfers between devices with their start and end apart: 4, of which 2 were waited for; matrix products, arithmetic and copies ran while one was open for 3% of the time, Pallas kernels for 0%

commit v1 on v0

--- a/solution.py
+++ b/solution.py
@@ -119,7 +119,7 @@
     )
     bias_part = jnp.sum(out_grad.astype(jnp.float32), axis=(0, 2, 3))
     factor = 1.0 / math.sqrt(local_members * owners * rows_out * lon_dev * lax.axis_size("lon"))
-    weight_sum, bias_sum = lax.psum((weight_part, bias_part), ("member", "lon"))
+    weight_sum, bias_sum = lax.psum(lax.psum((weight_part, bias_part), "lon"), "member")
     weight_grad = (weight_sum * factor).reshape(5, 5, out_chan, in_chan)
     bias_grad = bias_sum * factor
     return (out_grad, owned_score, weight_grad, bias_grad)

time: 311 us -> 396 us (1.27)
  waiting for transfers between devices: 100 us -> 200 us
  blocking collectives: 53.1 us -> 38.5 us
    psum x1 -> x2, waiting for transfers between devices: 95.6 us -> 195 us  [the longest x1 109 us: body(): lax.psum((weight_part, bias_part), 'lon')]
    psum x1 -> x2, blocking collectives: 38.1 us -> 22.5 us  [the longest x1 13.9 us: body(): lax.psum((weight_part, bias_part), 'lon')]
  transfers between devices with their start and end apart: 4 -> 5, of which waited for: 2 -> 3; matrix products, arithmetic and copies ran while one was open for 3% -> 2% of each run, Pallas kernels for 0% -> 0%
where the time goes in v1:
time: 396 us; the launch traced here: 394 us
  waiting for transfers between devices  200 us (51%)
  local copies, waits for them, and re-layouts  101 us (26%)
  blocking collectives  38.5 us (10%)
  other arithmetic  15.7 us (4%)
  matrix products  15.7 us (4%)
  between operations  14.3 us (4%)
  starting transfers between devices  8.83 us (2%)
    psum x1, waiting for transfers between devices, body(): lax.psum((weight_part, bias_part), 'lon')  109 us
    psum x1, waiting for transfers between devices, body(): lax.psum(lax.psum((weight_part, bias_part), 'lon'), 'member')  86.1 us
    slice x2, local copies, waits for them, and re-layouts, body(): tap_sums[:, row_tap, col_tap, :, row_tap:row_tap + rows_out, col_tap:col_...  31.4 us
    another operation x2, local copies, waits for them, and re-layouts  15.6 us
    reshape x1, local copies, waits for them, and re-layouts, body(): tap_sums.reshape(local_members, 5, 5, out_chan, rows_in, padded_width)  14.5 us
    psum x1, blocking collectives, body(): lax.psum((weight_part, bias_part), 'lon')  13.9 us
    transpose x1, local copies, waits for them, and re-layouts, body(): jnp.einsum('kc,mcp->mkp', flat_weight, flat_field, preferred_element_type...  8.69 us
    psum x1, blocking collectives, body(): lax.psum(lax.psum((weight_part, bias_part), 'lon'), 'member')  8.56 us
  transfers between devices with their start and end apart: 5, of which 3 were waited for; matrix products, arithmetic and copies ran while one was open for 2% of the time, Pallas kernels for 0%

profile of v1, /device:TPU:0, one launch (start us, length us, event | category | flops | bytes accessed | tf_op | source)
XLA Modules:
  0.0 394.2 jit_solution(2468471615739666669)
XLA Ops:
  7.2 1.2 fusion.72
  8.4 0.5 collective-permute-start
  8.9 4.1 %collective-permute-start.1 = (bf16[1,641,20,2]{1,3,2,0:T(2,128)(2,1)S(1)}, bf16[1,641,20,2]{1,3,2,0:T(2,128)(2,1)S(1)}, u32[]{:S(2)}, u32[]{:S(2)}) collective-permute-start(bf16[1,641,20,2]{1,3,2,0:T(2,128)(2,1)S(1)} %get-tuple-element.56), channel_id=1, source_target_pairs={{1,0},{2,1},{3,2},{4,3},{5,4},{6,5},{7,6},{0,7},{9,8},{10,9},{11,1... | collective-permute-start | bytes 153848 | tf_op jit(solution)/shard_map/ppermute | solution.py:19
  13.0 0.7 multiply_divide_fusion
  13.7 4.9 %reshape.609 = bf16[1825,641]{1,0:T(8,128)(2,1)} reshape(bf16[5,5,73,641]{3,2,1,0:T(8,128)(2,1)} %param.7) | data formatting | bytes 4679300 | tf_op jit(solution)/shard_map/reshape | solution.py:59
  18.6 2.4 pad_maximum_fusion
  21.0 1.9 reshape.608
  22.9 8.4 %convolution_bitcast_fusion = f32[1,1825,980]{2,1,0:T(8,128)} fusion(bf16[641,980]{0,1:T(8,128)(2,1)} %reshape.608, bf16[1825,641]{1,0:T(8,128)(2,1)} %reshape.609), kind=kOutput, calls=%fused_computation.1 | convolution fusion | flops 2292857088 | bytes 10750010 | tf_op jit(solution)/shard_map/kc,mcp->mkp/dot_general | solution.py:60
  31.2 8.7 %copy.47 = f32[1,1825,980]{1,2,0:T(8,128)} copy(f32[1,1825,980]{2,1,0:T(8,128)} %convolution_bitcast_fusion) | data formatting | bytes 14308000 | tf_op jit(solution)/shard_map/kc,mcp->mkp/transpose | solution.py:60
  39.9 14.5 %reshape.610 = f32[1,5,5,73,20,49]{3,2,1,5,4,0:T(8,128)} reshape(f32[1,1825,980]{1,2,0:T(8,128)} %copy.47) | data formatting | bytes 14308000 | tf_op jit(solution)/shard_map/reshape | solution.py:63
  54.5 22.3 %fusion.70 = (f32[1,1,1,73,16,45]{3,2,1,5,4,0:T(1,128)S(1)}, f32[1,1,1,73,16,45]{3,2,1,5,4,0:T(1,128)S(1)}, f32[1,1,1,73,16,45]{3,2,1,5,4,0:T(1,128)S(1)}, f32[1...) fusion(f32[1,5,5,73,20,49]{3,2,1,5,4,0:T(8,128)} %reshape.610), kind=kLoop, calls=%fused_computation.130 | loop fusion | bytes 7989120 | tf_op jit(solution)/shard_map/slice | solution.py:71
  76.8 9.1 %fusion.71 = (f32[1,1,1,73,16,45]{3,2,1,5,4,0:T(1,128)S(1)}, f32[1,1,1,73,16,45]{3,2,1,5,4,0:T(1,128)S(1)}, f32[1,1,1,73,16,45]{3,2,1,5,4,0:T(1,128)S(1)}, f32[1...) fusion(f32[1,5,5,73,20,49]{3,2,1,5,4,0:T(8,128)} %reshape.610), kind=kLoop, calls=%fused_computation.131 | loop fusion | bytes 2522880 | tf_op jit(solution)/shard_map/slice | solution.py:71
  85.9 3.6 add_convert_fusion
  89.5 1.0 copy.48
  90.4 4.2 %all-to-all-start = ((bf16[1,73,4,180]{3,1,0,2:T(8,128)(2,1)}), bf16[1,73,4,180]{3,1,0,2:T(8,128)(2,1)S(1)}, u32[]{:S(2)}, u32[]{:S(2)}) async-start(bf16[1,73,4,180]{3,1,0,2:T(8,128)(2,1)} %copy.48), calls=%async_computation | async-start | bytes 327680 | tf_op jit(solution)/shard_map/all_to_all | solution.py:92
  94.6 0.1 copy.62
  94.8 0.1 reshape.627
  94.9 4.8 %all-to-all-done = bf16[1,73,4,180]{3,1,0,2:T(8,128)(2,1)S(1)} async-done(((bf16[1,73,4,180]{3,1,0,2:T(8,128)(2,1)}), bf16[1,73,4,180]{3,1,0,2:T(8,128)(2,1)S(1)}, u32[]{:S(2)}, u32[]{:S(2)}) %all-to-all-start) | async-done | bytes 105152 | tf_op jit(solution)/shard_map/all_to_all | solution.py:92
  99.7 0.4 fusion.11
  100.2 1.6 fusion.3
  101.9 0.5 fusion.13
  102.4 7.8 %all_to_all.30 = bf16[4,73,1,180]{3,1,2,0:T(8,128)(2,1)S(1)} all-to-all(bf16[4,73,1,180]{3,1,2,0:T(8,128)(2,1)S(1)} %copy.54), channel_id=1, replica_groups=mesh['member'=4,'lon'=8] {'member'}, dimensions={0} | all-to-all | bytes 210240 | tf_op jit(solution)/shard_map/all_to_all | solution.py:98
  110.2 0.6 convert_reduce_fusion
  110.8 0.2 copy.56
  111.2 0.1 fusion.17
  111.3 0.1 fusion.19
  111.4 0.1 fusion.21
  111.5 0.1 fusion.23
  111.7 0.1 fusion.27
  111.8 0.1 fusion.29
  111.9 0.1 fusion.31
  112.0 0.1 fusion.33
  112.2 0.1 fusion.37
  112.3 0.1 fusion.39
  112.4 0.1 fusion.41
  112.5 0.1 fusion.43
  112.7 0.1 fusion.47
  112.8 0.1 fusion.49
  112.9 0.1 fusion.51
  113.0 0.1 fusion.53
  113.2 0.1 fusion.57
  113.3 0.1 fusion.59
  113.4 0.1 fusion.61
  113.5 0.1 fusion.63
  113.6 5.8 %copy.59 = bf16[1,25,73,20,49]{2,1,4,3,0:T(8,128)(2,1)} copy(bf16[1,25,73,20,49]{2,4,3,1,0:T(8,128)(2,1)S(1)} %fusion.63) | data formatting | bytes 7154000 | tf_op jit(solution)/shard_map/stack | solution.py:49
  119.5 13.7 %reshape.613 = bf16[1825,980]{0,1:T(8,128)(2,1)} reshape(bf16[1,25,73,20,49]{2,1,4,3,0:T(8,128)(2,1)} %copy.59) | data formatting | bytes 7154000 | tf_op jit(solution)/shard_map/reshape.9
  133.2 7.3 %fusion.73 = f32[1825,641]{0,1:T(8,128)} fusion(bf16[1825,980]{0,1:T(8,128)(2,1)} %reshape.613, bf16[641,980]{0,1:T(8,128)(2,1)S(1)} %copy-done.2), kind=kOutput, calls=%fused_computation.133 | convolution fusion | flops 2292857088 | bytes 9512660 | tf_op jit(solution)/shard_map/dot_general | solution.py:117
  140.6 109.0 %all-reduce.4.cloned.1.call-done = f32[1825,641]{0,1:T(8,128)} async-done(((f32[1825,641]{0,1:T(8,128)}), f32[1825,641]{0,1:T(8,128)}) %all-reduce.4.cloned.1.call-update) | async-done | bytes 4679316 | tf_op jit(solution)/shard_map/psum | solution.py:122
  249.8 0.1 min.9
  250.1 0.1 broadcast_in_dim.41
  250.3 0.1 broadcast_in_dim.43
  250.5 0.1 div.61
  250.5 0.6 gather_fusion
  251.1 0.1 gather.7
  251.3 8.1 %all_to_all.31 = f32[4,1,540]{2,1,0:T(1,128)S(1)} all-to-all(f32[4,1,540]{2,1,0:T(1,128)S(1)} %copy.58), channel_id=1, replica_groups=mesh['member'=4,'lon'=8] {'member'}, dimensions={0} | all-to-all | bytes 17280 | tf_op jit(solution)/shard_map/all_to_all | solution.py:109
  259.4 0.6 reshape.612
  260.0 0.7 copy.61
  260.7 13.9 %psum.30 = f32[73]{0:T(128)S(1)} all-reduce(f32[73]{0:T(128)S(1)} %get-tuple-element.26), channel_id=1, replica_groups=mesh['member'=4,'lon'=8] {'lon'}, use_global_device_ids=true, to_apply=%region_8.9 | all-reduce | flops 73 | bytes 584 | tf_op jit(solution)/shard_map/psum | solution.py:122
  274.7 8.6 %psum.31 = f32[73]{0:T(128)S(1)} all-reduce(f32[73]{0:T(128)S(1)} %psum.30), channel_id=1, replica_groups=mesh['member'=4,'lon'=8] {'member'}, use_global_device_ids=true, to_apply=%region_9.10 | all-reduce | flops 73 | bytes 584 | tf_op jit(solution)/shard_map/psum | solution.py:122
  283.2 0.5 broadcast_multiply_fusion.3
  283.8 86.1 %all-reduce.6.cloned.1.call-done = f32[1825,641]{0,1:T(8,128)} async-done(((f32[1825,641]{0,1:T(8,128)}), f32[1825,641]{0,1:T(8,128)}) %all-reduce.6.cloned.1.call-update) | async-done | bytes 4679316 | tf_op jit(solution)/shard_map/psum | solution.py:122
  369.9 5.1 %broadcast_multiply_fusion = f32[1825,641]{0,1:T(8,128)} fusion(f32[1825,641]{0,1:T(8,128)} %all-reduce.6.cloned.1.call-done), kind=kLoop, calls=%fused_computation.2 | loop fusion | flops 1169825 | bytes 9358600 | tf_op jit(solution)/shard_map/mul | solution.py:123
  375.0 6.1 %copy.60 = f32[1825,641]{1,0:T(8,128)} copy(f32[1825,641]{0,1:T(8,128)} %broadcast_multiply_fusion) | data formatting | bytes 9358600 | tf_op jit(solution)/shard_map/mul | solution.py:123
  381.1 6.2 %reshape.614 = f32[5,5,73,641]{3,2,1,0:T(8,128)} reshape(f32[1825,641]{1,0:T(8,128)} %copy.60) | data formatting | bytes 9358600 | tf_op jit(solution)/shard_map/reshape | solution.py:123
  (40 shorter events, 1.2 us)
Async XLA Ops:
  7.2 87.4 %copy-start = (f32[73,16,45]{0,1,2:T(8,128)S(1)}, f32[73,16,45]{0,1,2:T(8,128)}, u32[]{:S(2)}) copy-start(f32[73,16,45]{0,1,2:T(8,128)} %param.9) | copy-start | bytes 630724
  8.4 10.2 %collective-permute-start = (bf16[1,641,20,2]{1,3,2,0:T(2,128)(2,1)S(1)}, bf16[1,641,20,2]{1,3,2,0:T(2,128)(2,1)S(1)}, u32[]{:S(2)}, u32[]{:S(2)}) collective-permute-start(bf16[1,641,20,2]{1,3,2,0:T(2,128)(2,1)S(1)} %get-tuple-element.55), channel_id=1, source_target_pairs={{0,1},{1,2},{2,3},{3,4},{4,5},{5,6},{6,7},{7,0},{8,9},{9,10},{10,1... | collective-permute-start | bytes 153848 | tf_op jit(solution)/shard_map/ppermute | solution.py:16
  8.9 9.7 %collective-permute-start.1 = (bf16[1,641,20,2]{1,3,2,0:T(2,128)(2,1)S(1)}, bf16[1,641,20,2]{1,3,2,0:T(2,128)(2,1)S(1)}, u32[]{:S(2)}, u32[]{:S(2)}) collective-permute-start(bf16[1,641,20,2]{1,3,2,0:T(2,128)(2,1)S(1)} %get-tuple-element.56), channel_id=1, source_target_pairs={{1,0},{2,1},{3,2},{4,3},{5,4},{6,5},{7,6},{0,7},{9,8},{10,9},{11,1... | collective-permute-start | bytes 153848 | tf_op jit(solution)/shard_map/ppermute | solution.py:19
  54.5 31.4 %copy-start.3 = (f32[73]{0:T(128)S(1)}, f32[73]{0:T(128)}, u32[]{:S(2)}) copy-start(f32[73]{0:T(128)} %param.8) | copy-start | bytes 880
  90.4 9.3 %all-to-all-start = ((bf16[1,73,4,180]{3,1,0,2:T(8,128)(2,1)}), bf16[1,73,4,180]{3,1,0,2:T(8,128)(2,1)S(1)}, u32[]{:S(2)}, u32[]{:S(2)}) async-start(bf16[1,73,4,180]{3,1,0,2:T(8,128)(2,1)} %copy.48), calls=%async_computation | async-start | bytes 327680 | tf_op jit(solution)/shard_map/all_to_all | solution.py:92
  94.6 155.1 %all-reduce.4.cloned.1.call-start = ((), (), s32[]{:S(2)}) async-start(), calls=%async_computation.3 | async-start | bytes 9953280 | tf_op jit(solution)/shard_map/psum | solution.py:122
  119.5 13.7 %copy-start.2 = (bf16[641,980]{0,1:T(8,128)(2,1)S(1)}, bf16[641,980]{0,1:T(8,128)(2,1)}, u32[]{:S(2)}) copy-start(bf16[641,980]{0,1:T(8,128)(2,1)} %reshape.608) | copy-start | bytes 3769084
  140.5 109.1 %copy-start.4 = (s32[1,5]{1,0:T(1,128)S(1)}, s32[1,5]{1,0:T(1,128)}, u32[]{:S(2)}) copy-start(s32[1,5]{1,0:T(1,128)} %param.11) | copy-start | bytes 64
  140.6 229.3 %all-reduce.6.cloned.1.call-start = ((), (), s32[]{:S(2)}) async-start(), calls=%async_computation.4 | async-start | bytes 9953280 | tf_op jit(solution)/shard_map/psum | solution.py:122
  375.0 12.3 %copy-start.1 = (f32[73,16,45]{0,1,2:T(8,128)S(1)}, f32[73,16,45]{0,1,2:T(8,128)}, u32[]{:S(2)}) copy-start(f32[73,16,45]{0,1,2:T(8,128)} %param.9) | copy-start | bytes 630724
Sparse Core Ops, SparseCore 0:
  140.7 108.9 all-reduce.3
  253.0 116.8 all-reduce.5
